TPU v7x, 32 devices: a whole 2x2x4 slice. The times are simulated.
32 devices in a mesh: seq: 8 (over z, core), head: 4 (over y, x).
Axes of the slice: x: 2, y: 2, z: 4, core: 2. Of those that a mesh axis runs over, the one named last changes fastest.
Arguments:
- inputs: bfloat16 [2, 2048, 2048], P(None, ('seq', 'head')), may hold values from -6 to 6
- doc_lengths: int32 [2, 16], replicated, may hold values from 1 to 1920, 2048 in all within a row
- ln_gain: float32 [2048], P(('seq', 'head')), may hold values from 0.5 to 1.5
- ln_bias: float32 [2048], P(('seq', 'head')), may hold values from -1.25 to 1.25
- w_qkv: float32 [2048, 6144], P(('seq', 'head')), may hold values from -0.125 to 0.125
- b_qkv: float32 [6144], P(('seq', 'head')), may hold values from -0.1875 to 0.1875
- w_out: float32 [2048, 2048], P(('seq', 'head')), may hold values from -0.75 to 0.75
- b_out: float32 [2048], P(('seq', 'head')), may hold values from -1.25 to 1.25
- w_fc1: float32 [2048, 8192], P(('seq', 'head')), may hold values from -0.125 to 0.125
- b_fc1: float32 [8192], P(('seq', 'head')), may hold values from -1.75 to 1.75
- w_fc2: float32 [8192, 2048], P(('seq', 'head')), may hold values from -0.0625 to 0.0625
- b_fc2: float32 [2048], P(('seq', 'head')), may hold values from -1.25 to 1.25
- cotangent: bfloat16 [2, 2048, 2048], P(None, ('seq', 'head')), may hold values from -6 to 6
Outputs:
- output: bfloat16 [2, 2048, 2048], P(None, ('seq', 'head'))
- grad_input: bfloat16 [2, 2048, 2048], P(None, ('seq', 'head'))
- grad_ln_gain: float32 [2048], P(('seq', 'head'))
- grad_ln_bias: float32 [2048], P(('seq', 'head'))
- grad_w_qkv: float32 [2048, 6144], P(('seq', 'head'))
- grad_b_qkv: float32 [6144], P(('seq', 'head'))
- grad_w_out: float32 [2048, 2048], P(('seq', 'head'))
- grad_b_out: float32 [2048], P(('seq', 'head'))
- grad_w_fc1: float32 [2048, 8192], P(('seq', 'head'))
- grad_b_fc1: float32 [8192], P(('seq', 'head'))
- grad_w_fc2: float32 [8192, 2048], P(('seq', 'head'))
- grad_b_fc2: float32 [2048], P(('seq', 'head'))
Inputs may be any that keep to these rules, and one draw needn't show every extreme that they name: `doc_lengths`: in each row the lengths sum to 2048, and one document has exactly 1920 tokens.
All inputs are finite; a program needn't handle non-finite values.
Results may differ from a plain program's by a relative error of at most 0.011.
Values may be sent and summed in bfloat16 or wider, within the bound.
No kernel may reach another device: no remote copies, remote signals or barrier semaphores. Data moves between devices by JAX's collectives and lax.ppermute only.
A program may use at most 448 MiB of HBM per device.

v0:
```python
from functools import partial

import jax
import jax.numpy as jnp
from jax import lax
from jax.sharding import PartitionSpec as P

D = 2048
H = 32
HD = 64
ROT = 32


NEG_FILL = -1e30


def from_behind(block, axis, distance):
    devices = range(lax.axis_size(axis))
    route = [(i - distance, i) for i in devices if i - distance in devices]
    return lax.ppermute(block, axis, route)


def from_behind_2(shard, axis, by):
    length = lax.axis_size(axis)
    return lax.ppermute(shard, axis, [(i, (i + by) % length) for i in range(length)])


def rotate(field, cosine, sine):
    half_rot = ROT // 2
    first_part = field[..., :half_rot]
    second_part = field[..., half_rot:ROT]
    return jnp.concatenate(
        [
            first_part * cosine - second_part * sine,
            second_part * cosine + first_part * sine,
            field[..., ROT:],
        ],
        axis=-1,
    )


def rotation_tables(positions):
    half_rot = ROT // 2
    inverse = jnp.power(10000.0, -2.0 * jnp.arange(half_rot, dtype=jnp.float32) / ROT)
    angles = positions.astype(jnp.float32)[:, None] * inverse[None, :]
    return (jnp.cos(angles)[:, None, :], jnp.sin(angles)[:, None, :])


def layer_norm(values, gain_value, shift_value):
    center = values - jnp.mean(values, axis=-1, keepdims=True)
    spread = jnp.mean(center * center, axis=-1, keepdims=True)
    return center * lax.rsqrt(spread + 1e-05) * gain_value + shift_value


def segment_ids(doc_ends, positions):
    return jnp.sum((doc_ends[:, None, :] <= positions[None, :, None]).astype(jnp.int32), axis=2)


def gelu_tanh(values):
    return jax.nn.gelu(values, approximate=True)


def allowed_pairs(query_pos, query_seg, key_pos, key_seg):
    return (key_pos[None, :] <= query_pos[:, None]) & (key_seg[None, :] == query_seg[:, None])


def masked_scores(query_seq, key_seq, allowed):
    raw_scores = (
        jnp.einsum("qhd,khd->hqk", query_seq, key_seq, preferred_element_type=jnp.float32) * 0.125
    )
    return jnp.where(allowed[None], raw_scores, NEG_FILL)


def forward_step(members, query_pos, key_pos):
    top_val, total_val, accum_val, query_seq, kv_seq, query_seg, key_seg = members
    kv_split = kv_seq.reshape(kv_seq.shape[0], 2, -1, HD)
    allowed = allowed_pairs(query_pos, query_seg, key_pos, key_seg)
    masked = masked_scores(query_seq, kv_split[:, 0], allowed)
    new_top = jnp.maximum(top_val, jnp.max(masked, axis=2))
    weights = jnp.where(allowed[None], jnp.exp(masked - new_top[:, :, None]), 0.0)
    factor = jnp.exp(top_val - new_top)
    new_total = total_val * factor + jnp.sum(weights, axis=2)
    new_accum = accum_val * factor[:, :, None] + jnp.einsum(
        "hqk,khd->hqd",
        weights.astype(jnp.bfloat16),
        kv_split[:, 1],
        preferred_element_type=jnp.float32,
    )
    return (new_top, new_total, new_accum)


def backward_step(members, query_pos, key_pos):
    grad_query, grad_kv, query_seq, kv_seq, grad_att, log_total, row_dot, query_seg, key_seg = (
        members
    )
    key_total = kv_seq.shape[0]
    kv_split = kv_seq.reshape(key_total, 2, -1, HD)
    allowed = allowed_pairs(query_pos, query_seg, key_pos, key_seg)
    masked = masked_scores(query_seq, kv_split[:, 0], allowed)
    prob_full = jnp.where(allowed[None], jnp.exp(masked - log_total[:, :, None]), 0.0)
    grad_value = jnp.einsum(
        "hqk,qhd->khd", prob_full.astype(jnp.bfloat16), grad_att, preferred_element_type=jnp.float32
    )
    grad_probs = jnp.einsum(
        "qhd,khd->hqk", grad_att, kv_split[:, 1], preferred_element_type=jnp.float32
    )
    grad_scores = (prob_full * (grad_probs - row_dot[:, :, None])).astype(jnp.bfloat16)
    grad_query = (
        grad_query
        + jnp.einsum(
            "hqk,khd->hqd", grad_scores, kv_split[:, 0], preferred_element_type=jnp.float32
        )
        * 0.125
    )
    grad_key = (
        jnp.einsum("hqk,qhd->khd", grad_scores, query_seq, preferred_element_type=jnp.float32)
        * 0.125
    )
    grad_kv = grad_kv + jnp.stack([grad_key, grad_value], axis=1).reshape(key_total, 2, -1)
    return (grad_query, grad_kv)


def per_device(
    inputs,
    doc_lengths,
    ln_gain,
    ln_bias,
    w_qkv,
    b_qkv,
    w_out,
    b_out,
    w_fc1,
    b_fc1,
    w_fc2,
    b_fc2,
    cotangent,
):
    seq_total = inputs.shape[0]
    row_count = inputs.shape[1]
    head_count = lax.axis_size("head")
    seq_devices = lax.axis_size("seq")
    heads_here = H // head_count
    group_width = heads_here * HD
    block_rows = row_count * head_count
    seq_rank = lax.axis_index("seq")
    head_rank = lax.axis_index("head")
    doc_ends = jnp.cumsum(doc_lengths, axis=1)
    token_pos = (seq_rank * head_count + head_rank) * row_count + jnp.arange(
        row_count, dtype=jnp.int32
    )
    query_start = seq_rank * block_rows
    query_pos = query_start + jnp.arange(block_rows, dtype=jnp.int32)
    query_seg = segment_ids(doc_ends, query_pos)
    gathered = (
        lax.all_gather(ln_gain.astype(jnp.bfloat16), ("seq", "head"), axis=0, tiled=True),
        lax.all_gather(ln_bias.astype(jnp.bfloat16), ("seq", "head"), axis=0, tiled=True),
        lax.all_gather(w_qkv.astype(jnp.bfloat16), ("seq", "head"), axis=0, tiled=True),
        lax.all_gather(b_qkv.astype(jnp.bfloat16), ("seq", "head"), axis=0, tiled=True),
        lax.all_gather(w_out.astype(jnp.bfloat16), ("seq", "head"), axis=0, tiled=True),
        lax.all_gather(b_out.astype(jnp.bfloat16), ("seq", "head"), axis=0, tiled=True),
        lax.all_gather(w_fc1.astype(jnp.bfloat16), ("seq", "head"), axis=0, tiled=True),
        lax.all_gather(b_fc1.astype(jnp.bfloat16), ("seq", "head"), axis=0, tiled=True),
        lax.all_gather(w_fc2.astype(jnp.bfloat16), ("seq", "head"), axis=0, tiled=True),
        lax.all_gather(b_fc2.astype(jnp.bfloat16), ("seq", "head"), axis=0, tiled=True),
    )
    (
        gain_full,
        shift_full,
        qkv_weight,
        qkv_bias,
        out_weight,
        out_bias,
        up_weight,
        up_bias,
        down_weight,
        down_bias,
    ) = gathered
    flat_in = inputs.reshape(seq_total * row_count, D).astype(jnp.float32)
    normed, norm_back = jax.vjp(
        layer_norm, flat_in, gain_full.astype(jnp.float32), shift_full.astype(jnp.float32)
    )
    normed_low = normed.astype(jnp.bfloat16)
    qkv_all = (
        jnp.dot(normed_low, qkv_weight, preferred_element_type=jnp.float32)
        + qkv_bias.astype(jnp.float32)
    ).reshape(seq_total, row_count, 3, H, HD)
    cosine, sine = rotation_tables(token_pos)

    def turn_field(field):
        return rotate(field, cosine, sine)

    query_rot, turn_back = jax.vjp(turn_field, qkv_all[:, :, 0])
    key_rot = turn_field(qkv_all[:, :, 1])
    stacked = (
        jnp.stack([query_rot, key_rot, qkv_all[:, :, 2]], axis=2)
        .reshape(seq_total, row_count, 3, D)
        .astype(jnp.bfloat16)
    )
    by_heads = lax.all_to_all(stacked, "head", split_axis=3, concat_axis=1, tiled=True)
    query_heads = by_heads[:, :, 0].reshape(seq_total, block_rows, heads_here, HD)
    kv_heads = by_heads[:, :, 1:3]
    start_state = (
        jnp.full((seq_total, heads_here, block_rows), NEG_FILL, jnp.float32),
        jnp.zeros((seq_total, heads_here, block_rows), jnp.float32),
        jnp.zeros((seq_total, heads_here, block_rows, HD), jnp.float32),
    )
    shard_piece = lax.all_gather(kv_heads, "seq", axis=1, tiled=True)

    def one_turn(turn_index, current):
        kv_block = lax.dynamic_slice_in_dim(shard_piece, turn_index * block_rows, block_rows, 1)
        key_start = turn_index * block_rows
        key_pos = key_start + jnp.arange(block_rows, dtype=jnp.int32)
        key_seg = segment_ids(doc_ends, key_pos)

        def one_compute(state_in):
            return lax.map(
                partial(forward_step, query_pos=query_pos, key_pos=key_pos),
                (state_in[0], state_in[1], state_in[2], query_heads, kv_block, query_seg, key_seg),
            )

        return lax.cond(
            key_start < query_start + block_rows, one_compute, lambda state_in: state_in, current
        )

    top_all, total_all, accum_all = lax.fori_loop(
        0, shard_piece.shape[1] // block_rows, one_turn, start_state
    )
    attn_full = accum_all / total_all[:, :, :, None]
    log_total = top_all + jnp.log(total_all)
    attn_low = (
        jnp.transpose(attn_full, (0, 2, 1, 3))
        .reshape(seq_total, block_rows, group_width)
        .astype(jnp.bfloat16)
    )
    attended = lax.all_to_all(attn_low, "head", split_axis=1, concat_axis=2, tiled=True).reshape(
        seq_total * row_count, D
    )
    branch = jnp.dot(attended, out_weight, preferred_element_type=jnp.float32) + out_bias.astype(
        jnp.float32
    )
    hidden = jnp.dot(normed_low, up_weight, preferred_element_type=jnp.float32) + up_bias.astype(
        jnp.float32
    )
    active, gelu_back = jax.vjp(gelu_tanh, hidden)
    active_low = active.astype(jnp.bfloat16)
    feed = jnp.dot(active_low, down_weight, preferred_element_type=jnp.float32) + down_bias.astype(
        jnp.float32
    )
    output = (flat_in + branch + feed).astype(jnp.bfloat16).reshape(inputs.shape)
    qkv_weight, out_weight, up_weight, down_weight = (
        lax.all_gather(w_qkv.astype(jnp.bfloat16), ("seq", "head"), axis=0, tiled=True),
        lax.all_gather(w_out.astype(jnp.bfloat16), ("seq", "head"), axis=0, tiled=True),
        lax.all_gather(w_fc1.astype(jnp.bfloat16), ("seq", "head"), axis=0, tiled=True),
        lax.all_gather(w_fc2.astype(jnp.bfloat16), ("seq", "head"), axis=0, tiled=True),
    )
    grad_low = cotangent.reshape(seq_total * row_count, D)
    grad_full = grad_low.astype(jnp.float32)
    cot_sum = jnp.sum(grad_full, axis=0)
    grad_down_w = jnp.einsum("nf,nd->fd", active_low, grad_low, preferred_element_type=jnp.float32)
    grad_active = jnp.einsum("nd,fd->nf", grad_low, down_weight, preferred_element_type=jnp.float32)
    grad_hidden_low = gelu_back(grad_active)[0].astype(jnp.bfloat16)
    grad_up_w = jnp.einsum(
        "nm,nf->mf", normed_low, grad_hidden_low, preferred_element_type=jnp.float32
    )
    grad_up_b = jnp.sum(grad_hidden_low.astype(jnp.float32), axis=0)
    grad_normed = jnp.einsum(
        "nf,mf->nm", grad_hidden_low, up_weight, preferred_element_type=jnp.float32
    )
    grad_out_w = jnp.einsum("nm,nd->md", attended, grad_low, preferred_element_type=jnp.float32)
    grad_att_low = jnp.einsum(
        "nd,md->nm", grad_low, out_weight, preferred_element_type=jnp.float32
    ).astype(jnp.bfloat16)
    grad_heads = lax.all_to_all(
        grad_att_low.reshape(seq_total, row_count, D),
        "head",
        split_axis=2,
        concat_axis=1,
        tiled=True,
    ).reshape(seq_total, block_rows, heads_here, HD)
    row_dot = jnp.sum(
        jnp.transpose(grad_heads.astype(jnp.float32), (0, 2, 1, 3)) * attn_full, axis=3
    )

    def back_turn(turn_index, current):
        grad_query, grad_kv, kv_now = current
        source = (seq_rank - turn_index) % seq_devices
        key_pos = source * block_rows + jnp.arange(block_rows, dtype=jnp.int32)
        key_seg = segment_ids(doc_ends, key_pos)

        def back_compute(grads_in):
            return lax.map(
                partial(backward_step, query_pos=query_pos, key_pos=key_pos),
                (
                    grads_in[0],
                    grads_in[1],
                    query_heads,
                    kv_now,
                    grad_heads,
                    log_total,
                    row_dot,
                    query_seg,
                    key_seg,
                ),
            )

        return lax.cond(
            source <= seq_rank, back_compute, lambda grads_in: grads_in, (grad_query, grad_kv)
        )

    def pass_keys(kv_now):
        return from_behind(kv_now, "seq", 1)

    def pass_grads(grad_kv):
        return from_behind_2(grad_kv.astype(jnp.bfloat16), "seq", 1).astype(grad_kv.dtype)

    def loop_turn(turn_index, current):
        grad_query, grad_kv = back_turn(turn_index, current)
        return (grad_query, pass_grads(grad_kv), pass_keys(current[2]))

    start_grads = (
        jnp.zeros((seq_total, heads_here, block_rows, HD), jnp.float32),
        jnp.zeros((seq_total, block_rows, 2, group_width), jnp.float32),
        kv_heads,
    )
    loop_state = lax.fori_loop(0, seq_devices - 1, loop_turn, start_grads)
    grad_query, grad_kv = back_turn(seq_devices - 1, loop_state)
    grad_kv = pass_grads(grad_kv)
    back_heads = jnp.concatenate(
        [
            jnp.transpose(grad_query, (0, 2, 1, 3)).reshape(seq_total, block_rows, 1, group_width),
            grad_kv,
        ],
        axis=2,
    ).astype(jnp.bfloat16)
    back_tokens = (
        lax.all_to_all(back_heads, "head", split_axis=1, concat_axis=3, tiled=True)
        .astype(jnp.float32)
        .reshape(seq_total, row_count, 3, H, HD)
    )
    grad_qkv_low = (
        jnp.stack(
            [
                turn_back(back_tokens[:, :, 0])[0],
                turn_back(back_tokens[:, :, 1])[0],
                back_tokens[:, :, 2],
            ],
            axis=2,
        )
        .reshape(seq_total * row_count, 3 * D)
        .astype(jnp.bfloat16)
    )
    grad_qkv_w = jnp.einsum(
        "nm,nk->mk", normed_low, grad_qkv_low, preferred_element_type=jnp.float32
    )
    grad_qkv_b = jnp.sum(grad_qkv_low.astype(jnp.float32), axis=0)
    grad_normed = grad_normed + jnp.einsum(
        "nk,mk->nm", grad_qkv_low, qkv_weight, preferred_element_type=jnp.float32
    )
    grad_in, grad_gain, grad_shift = norm_back(grad_normed)
    grad_input = (grad_full + grad_in).astype(jnp.bfloat16).reshape(inputs.shape)
    sums_all = (
        lax.psum_scatter(grad_gain, ("seq", "head"), scatter_dimension=0, tiled=True),
        lax.psum_scatter(grad_shift, ("seq", "head"), scatter_dimension=0, tiled=True),
        lax.psum_scatter(grad_qkv_w, ("seq", "head"), scatter_dimension=0, tiled=True),
        lax.psum_scatter(grad_qkv_b, ("seq", "head"), scatter_dimension=0, tiled=True),
        lax.psum_scatter(grad_out_w, ("seq", "head"), scatter_dimension=0, tiled=True),
        lax.psum_scatter(cot_sum, ("seq", "head"), scatter_dimension=0, tiled=True),
        lax.psum_scatter(grad_up_w, ("seq", "head"), scatter_dimension=0, tiled=True),
        lax.psum_scatter(grad_up_b, ("seq", "head"), scatter_dimension=0, tiled=True),
        lax.psum_scatter(grad_down_w, ("seq", "head"), scatter_dimension=0, tiled=True),
    )
    return (
        output,
        grad_input,
        sums_all[0],
        sums_all[1],
        sums_all[2],
        sums_all[3],
        sums_all[4],
        sums_all[5],
        sums_all[6],
        sums_all[7],
        sums_all[8],
        sums_all[5],
    )


def solution(mesh):
    return jax.shard_map(
        per_device,
        mesh=mesh,
        in_specs=(
            P(None, ("seq", "head"), None),
            P(),
            P(("seq", "head")),
            P(("seq", "head")),
            P(("seq", "head"), None),
            P(("seq", "head")),
            P(("seq", "head"), None),
            P(("seq", "head")),
            P(("seq", "head"), None),
            P(("seq", "head")),
            P(("seq", "head"), None),
            P(("seq", "head")),
            P(None, ("seq", "head"), None),
        ),
        out_specs=(
            P(None, ("seq", "head"), None),
            P(None, ("seq", "head"), None),
            P(("seq", "head")),
            P(("seq", "head")),
            P(("seq", "head"), None),
            P(("seq", "head")),
            P(("seq", "head"), None),
            P(("seq", "head")),
            P(("seq", "head"), None),
            P(("seq", "head")),
            P(("seq", "head"), None),
            P(("seq", "head")),
        ),
        check_vma=False,
    )
```

profile of v0, /device:TPU:0, one launch (start us, length us, event | category | flops | bytes accessed | tf_op | source)
XLA Modules:
  0.0 4819.1 jit_solution(7159399987818747255)
XLA Ops:
  12.0 44.3 all-reduce.17
  59.0 111.4 %all-gather.7.cloned.1.call-done = bf16[2048,6144]{1,0:T(8,128)(2,1)} async-done(((bf16[64,6144]{1,0:T(8,128)(2,1)}), bf16[2048,6144]{1,0:T(8,128)(2,1)}) %all-gather.7.cloned.1.call-update) | async-done | bytes 25165840 | tf_op jit(solution)/shard_map/all_gather | solution.py:157
  216.4 37.9 all_to_all.57
  285.6 68.7 %all-gather = bf16[32,1,256]{2,1,0:T(2,128)(2,1)S(1)} all-gather(bf16[1,1,256]{2,1,0:T(2,128)(2,1)S(1)} %reshape.494), channel_id=1, replica_groups=mesh['seq'=8,'head'=4] {'seq','head'}, dimensions={0}, use_global_device_ids=true | all-gather | bytes 16896 | tf_op jit(solution)/shard_map/all_gather | solution.py:162
  399.9 525.5 %while.89 = (s32[]{:T(128)}, f32[2,8,256,64]{2,3,1,0:T(8,128)}, f32[2,256,2,512]{1,3,2,0:T(8,128)}, bf16[2,256,2,512]{1,3,2,0:T(8,128)(2,1)}, s32[]{:T(128)}, /*...) while((s32[]{:T(128)}, f32[2,8,256,64]{2,3,1,0:T(8,128)}, ...), condition=%wide.region_20.21_spmd.clone, body=%wide.region_14.20_spmd.clone.sunk | while | flops 342450464 | bytes 91228328 | solution.py:325
  427.7 72.6 %collective-permute-done = bf16[2,256,2,512]{1,3,2,0:T(8,128)(2,1)S(1)} collective-permute-done((bf16[2,256,2,512]{1,3,2,0:T(8,128)(2,1)}, bf16[2,256,2,512]{1,3,2,0:T(8,128)(2,1)S(1)}, u32[]{:S(2)}, u32[]{:S(2)}) %collective-permute-start) | collective-permute-done | bytes 1048608 | tf_op jit(solution)/shard_map/while/body/eval_jaxpr/ppermute | solution.py:25
  507.8 50.0 %collective-permute-done = bf16[2,256,2,512]{1,3,2,0:T(8,128)(2,1)S(1)} collective-permute-done((bf16[2,256,2,512]{1,3,2,0:T(8,128)(2,1)}, bf16[2,256,2,512]{1,3,2,0:T(8,128)(2,1)S(1)}, u32[]{:S(2)}, u32[]{:S(2)}) %collective-permute-start) | collective-permute-done | bytes 1048608 | tf_op jit(solution)/shard_map/while/body/eval_jaxpr/ppermute | solution.py:25
  575.8 23.2 collective-permute-start.1
  599.0 31.2 collective-permute-done
  657.6 31.0 collective-permute-done
  693.9 25.1 collective-permute-start
  724.3 57.5 %collective-permute-done = bf16[2,256,2,512]{1,3,2,0:T(8,128)(2,1)S(1)} collective-permute-done((bf16[2,256,2,512]{1,3,2,0:T(8,128)(2,1)}, bf16[2,256,2,512]{1,3,2,0:T(8,128)(2,1)S(1)}, u32[]{:S(2)}, u32[]{:S(2)}) %collective-permute-start) | collective-permute-done | bytes 1048608 | tf_op jit(solution)/shard_map/while/body/eval_jaxpr/ppermute | solution.py:25
  787.0 34.5 collective-permute-start
  827.1 49.6 %collective-permute-done = bf16[2,256,2,512]{1,3,2,0:T(8,128)(2,1)S(1)} collective-permute-done((bf16[2,256,2,512]{1,3,2,0:T(8,128)(2,1)}, bf16[2,256,2,512]{1,3,2,0:T(8,128)(2,1)S(1)}, u32[]{:S(2)}, u32[]{:S(2)}) %collective-permute-start) | collective-permute-done | bytes 1048608 | tf_op jit(solution)/shard_map/while/body/eval_jaxpr/ppermute | solution.py:25
  884.2 39.6 collective-permute-done
  948.3 18.5 convert_reduce_fusion.1
  1056.8 20.4 fusion.80
  1078.2 25.1 fusion.82
  1103.5 25.4 fusion.74
  1153.4 42.5 all-reduce.20.cloned.1.call-done
  1201.9 355.9 %reduce-scatter.7.cloned.1.call-done = f32[64,2048]{1,0:T(8,128)} async-done(((f32[2048,2048]{1,0:T(8,128)}), f32[64,2048]{1,0:T(8,128)}) %reduce-scatter.7.cloned.1.call-update) | async-done | bytes 524304 | tf_op jit(solution)/shard_map/reduce_scatter | solution.py:366
  1557.8 440.0 %reduce-scatter.5.cloned.1.call-done = f32[64,6144]{1,0:T(8,128)} async-done(((f32[2048,6144]{1,0:T(8,128)}), f32[64,6144]{1,0:T(8,128)}) %reduce-scatter.5.cloned.1.call-update) | async-done | bytes 1572880 | tf_op jit(solution)/shard_map/reduce_scatter | solution.py:364
  1997.8 1406.3 %reduce-scatter.9.cloned.1.call-done = f32[64,8192]{1,0:T(8,128)} async-done(((f32[2048,8192]{1,0:T(8,128)}), f32[64,8192]{1,0:T(8,128)}) %reduce-scatter.9.cloned.1.call-update) | async-done | bytes 2097168 | tf_op jit(solution)/shard_map/reduce_scatter | solution.py:368
  3404.2 1407.3 %reduce-scatter.11.cloned.1.call-done = f32[256,2048]{1,0:T(8,128)} async-done(((f32[8192,2048]{1,0:T(8,128)}), f32[256,2048]{1,0:T(8,128)}) %reduce-scatter.11.cloned.1.call-update) | async-done | bytes 2097168 | tf_op jit(solution)/shard_map/reduce_scatter | solution.py:370
  (451 shorter events, 435.6 us)
Async XLA Ops:
  7.3 163.2 %all-gather.7.cloned.1.call-start = ((), (), s32[]{:S(2)}) async-start(), calls=%async_computation.8 | async-start | bytes 25952256 | tf_op jit(solution)/shard_map/all_gather | solution.py:157
  9.8 263.0 %all-gather.11.cloned.1.call-start = ((), (), s32[]{:S(2)}) async-start(), calls=%async_computation.10 | async-start | bytes 8650752 | tf_op jit(solution)/shard_map/all_gather | solution.py:159
  10.6 353.2 %all-gather.9.cloned.1.call-start = ((), (), s32[]{:S(2)}) async-start(), calls=%async_computation.9 | async-start | bytes 9437184 | tf_op jit(solution)/shard_map/all_gather | solution.py:207
  268.4 662.4 %all-gather.15.cloned.1.call-start = ((), (), s32[]{:S(2)}) async-start(), calls=%async_computation.12 | async-start | bytes 34603008 | tf_op jit(solution)/shard_map/all_gather | solution.py:163
  269.7 678.6 %all-gather.13.cloned.1.call-start = ((), (), s32[]{:S(2)}) async-start(), calls=%async_computation.11 | async-start | bytes 34603008 | tf_op jit(solution)/shard_map/all_gather | solution.py:161
  282.1 74.3 %all-to-all-start.2 = ((bf16[4,2,32768]{2,1,0:T(2,128)(2,1)}), bf16[4,2,32768]{2,1,0:T(2,128)(2,1)S(1)}, u32[]{:S(2)}, u32[]{:S(2)}) async-start(bf16[4,2,32768]{2,1,0:T(2,128)(2,1)} %reshape.499), calls=%async_computation.2 | async-start | bytes 1048576 | tf_op jit(solution)/shard_map/all_to_all | solution.py:273
  384.2 591.8 %all-to-all-start.1 = ((bf16[2,256,512]{2,0,1:T(2,128)(2,1)}), bf16[2,256,512]{2,0,1:T(2,128)(2,1)}, u32[]{:S(2)}, u32[]{:S(2)}) async-start(bf16[2,256,512]{2,0,1:T(2,128)(2,1)} %copy.133), calls=%async_computation.1 | async-start | bytes 1048576 | tf_op jit(solution)/shard_map/all_to_all | solution.py:235
  421.2 79.1 %collective-permute-start = (bf16[2,256,2,512]{1,3,2,0:T(8,128)(2,1)}, bf16[2,256,2,512]{1,3,2,0:T(8,128)(2,1)S(1)}, u32[]{:S(2)}, u32[]{:S(2)}) collective-permute-start(bf16[2,256,2,512]{1,3,2,0:T(8,128)(2,1)} %convert_element_type.347), channel_id=1, source_target_pairs={{0,4},{4,8},{8,12},{12,16},{16,20},{20,24},{24,28},{28,0},{1,5},{5... | collective-permute-start | bytes 3145736 | tf_op jit(solution)/shard_map/while/body/eval_jaxpr/ppermute | solution.py:25
  423.0 78.8 %collective-permute-start.1 = (bf16[2,256,2,512]{1,3,2,0:T(8,128)(2,1)}, bf16[2,256,2,512]{1,3,2,0:T(8,128)(2,1)}, u32[]{:S(2)}, u32[]{:S(2)}) collective-permute-start(bf16[2,256,2,512]{1,3,2,0:T(8,128)(2,1)} %copy.234), channel_id=1, source_target_pairs={{0,4},{4,8},{8,12},{12,16},{16,20},{20,24},{24,28},{1,5},{5,9},{9,... | collective-permute-start | bytes 3145736 | tf_op jit(solution)/shard_map/while/body/eval_jaxpr/ppermute | solution.py:20
  505.6 52.2 %collective-permute-start = (bf16[2,256,2,512]{1,3,2,0:T(8,128)(2,1)}, bf16[2,256,2,512]{1,3,2,0:T(8,128)(2,1)S(1)}, u32[]{:S(2)}, u32[]{:S(2)}) collective-permute-start(bf16[2,256,2,512]{1,3,2,0:T(8,128)(2,1)} %convert_element_type.347), channel_id=1, source_target_pairs={{0,4},{4,8},{8,12},{12,16},{16,20},{20,24},{24,28},{28,0},{1,5},{5... | collective-permute-start | bytes 3145736 | tf_op jit(solution)/shard_map/while/body/eval_jaxpr/ppermute | solution.py:25
  505.6 53.8 %collective-permute-start.1 = (bf16[2,256,2,512]{1,3,2,0:T(8,128)(2,1)}, bf16[2,256,2,512]{1,3,2,0:T(8,128)(2,1)}, u32[]{:S(2)}, u32[]{:S(2)}) collective-permute-start(bf16[2,256,2,512]{1,3,2,0:T(8,128)(2,1)} %copy.234), channel_id=1, source_target_pairs={{0,4},{4,8},{8,12},{12,16},{16,20},{20,24},{24,28},{1,5},{5,9},{9,... | collective-permute-start | bytes 3145736 | tf_op jit(solution)/shard_map/while/body/eval_jaxpr/ppermute | solution.py:20
  563.2 67.0 %collective-permute-start = (bf16[2,256,2,512]{1,3,2,0:T(8,128)(2,1)}, bf16[2,256,2,512]{1,3,2,0:T(8,128)(2,1)S(1)}, u32[]{:S(2)}, u32[]{:S(2)}) collective-permute-start(bf16[2,256,2,512]{1,3,2,0:T(8,128)(2,1)} %convert_element_type.347), channel_id=1, source_target_pairs={{0,4},{4,8},{8,12},{12,16},{16,20},{20,24},{24,28},{28,0},{1,5},{5... | collective-permute-start | bytes 3145736 | tf_op jit(solution)/shard_map/while/body/eval_jaxpr/ppermute | solution.py:25
  575.8 55.9 %collective-permute-start.1 = (bf16[2,256,2,512]{1,3,2,0:T(8,128)(2,1)}, bf16[2,256,2,512]{1,3,2,0:T(8,128)(2,1)}, u32[]{:S(2)}, u32[]{:S(2)}) collective-permute-start(bf16[2,256,2,512]{1,3,2,0:T(8,128)(2,1)} %copy.234), channel_id=1, source_target_pairs={{0,4},{4,8},{8,12},{12,16},{16,20},{20,24},{24,28},{1,5},{5,9},{9,... | collective-permute-start | bytes 3145736 | tf_op jit(solution)/shard_map/while/body/eval_jaxpr/ppermute | solution.py:20
  635.7 52.9 %collective-permute-start = (bf16[2,256,2,512]{1,3,2,0:T(8,128)(2,1)}, bf16[2,256,2,512]{1,3,2,0:T(8,128)(2,1)S(1)}, u32[]{:S(2)}, u32[]{:S(2)}) collective-permute-start(bf16[2,256,2,512]{1,3,2,0:T(8,128)(2,1)} %convert_element_type.347), channel_id=1, source_target_pairs={{0,4},{4,8},{8,12},{12,16},{16,20},{20,24},{24,28},{28,0},{1,5},{5... | collective-permute-start | bytes 3145736 | tf_op jit(solution)/shard_map/while/body/eval_jaxpr/ppermute | solution.py:25
  693.9 87.9 %collective-permute-start = (bf16[2,256,2,512]{1,3,2,0:T(8,128)(2,1)}, bf16[2,256,2,512]{1,3,2,0:T(8,128)(2,1)S(1)}, u32[]{:S(2)}, u32[]{:S(2)}) collective-permute-start(bf16[2,256,2,512]{1,3,2,0:T(8,128)(2,1)} %convert_element_type.347), channel_id=1, source_target_pairs={{0,4},{4,8},{8,12},{12,16},{16,20},{20,24},{24,28},{28,0},{1,5},{5... | collective-permute-start | bytes 3145736 | tf_op jit(solution)/shard_map/while/body/eval_jaxpr/ppermute | solution.py:25
  719.0 64.3 %collective-permute-start.1 = (bf16[2,256,2,512]{1,3,2,0:T(8,128)(2,1)}, bf16[2,256,2,512]{1,3,2,0:T(8,128)(2,1)}, u32[]{:S(2)}, u32[]{:S(2)}) collective-permute-start(bf16[2,256,2,512]{1,3,2,0:T(8,128)(2,1)} %copy.234), channel_id=1, source_target_pairs={{0,4},{4,8},{8,12},{12,16},{16,20},{20,24},{24,28},{1,5},{5,9},{9,... | collective-permute-start | bytes 3145736 | tf_op jit(solution)/shard_map/while/body/eval_jaxpr/ppermute | solution.py:20
  787.0 89.7 %collective-permute-start = (bf16[2,256,2,512]{1,3,2,0:T(8,128)(2,1)}, bf16[2,256,2,512]{1,3,2,0:T(8,128)(2,1)S(1)}, u32[]{:S(2)}, u32[]{:S(2)}) collective-permute-start(bf16[2,256,2,512]{1,3,2,0:T(8,128)(2,1)} %convert_element_type.347), channel_id=1, source_target_pairs={{0,4},{4,8},{8,12},{12,16},{16,20},{20,24},{24,28},{28,0},{1,5},{5... | collective-permute-start | bytes 3145736 | tf_op jit(solution)/shard_map/while/body/eval_jaxpr/ppermute | solution.py:25
  821.5 56.7 %collective-permute-start.1 = (bf16[2,256,2,512]{1,3,2,0:T(8,128)(2,1)}, bf16[2,256,2,512]{1,3,2,0:T(8,128)(2,1)}, u32[]{:S(2)}, u32[]{:S(2)}) collective-permute-start(bf16[2,256,2,512]{1,3,2,0:T(8,128)(2,1)} %copy.234), channel_id=1, source_target_pairs={{0,4},{4,8},{8,12},{12,16},{16,20},{20,24},{24,28},{1,5},{5,9},{9,... | collective-permute-start | bytes 3145736 | tf_op jit(solution)/shard_map/while/body/eval_jaxpr/ppermute | solution.py:20
  882.0 43.4 collective-permute-start.1
  980.4 215.6 %all-reduce.20.cloned.1.call-start = ((), (), s32[]{:S(2)}) async-start(), calls=%async_computation.17 | async-start | bytes 163840
  1046.7 511.1 %reduce-scatter.7.cloned.1.call-start = ((), (), s32[]{:S(2)}) async-start(), calls=%async_computation.14 | async-start | bytes 17301504 | tf_op jit(solution)/shard_map/reduce_scatter | solution.py:366
  1055.0 942.8 %reduce-scatter.5.cloned.1.call-start = ((), (), s32[]{:S(2)}) async-start(), calls=%async_computation.13 | async-start | bytes 51904512 | tf_op jit(solution)/shard_map/reduce_scatter | solution.py:364
  1077.2 2326.9 %reduce-scatter.9.cloned.1.call-start = ((), (), s32[]{:S(2)}) async-start(), calls=%async_computation.15 | async-start | bytes 69206016 | tf_op jit(solution)/shard_map/reduce_scatter | solution.py:368
  1103.4 3708.1 %reduce-scatter.11.cloned.1.call-start = ((), (), s32[]{:S(2)}) async-start(), calls=%async_computation.16 | async-start | bytes 69206016 | tf_op jit(solution)/shard_map/reduce_scatter | solution.py:370
  (71 other events, 5373.6 us)
Sparse Core Ops, SparseCore 0:
  11.5 158.8 all-gather.6
  173.9 91.7 all-gather.10
  268.5 81.6 all-gather.8
  352.9 225.4 all-gather.14
  581.1 236.3 all-gather.12
  1046.8 149.0 all-reduce.19
  1198.8 358.9 reduce-scatter.6
  1564.8 432.9 reduce-scatter.4
  2000.8 1403.3 reduce-scatter.8
  3406.9 1404.5 reduce-scatter.10
where the time goes:
time: 4810 us; the launch traced here: 4820 us
  waiting for transfers between devices  4100 us (85%)
  matrix products  195 us (4%)
  starting transfers between devices  162 us (3%)
  blocking collectives  151 us (3%)
  local copies, waits for them, and re-layouts  137 us (3%)
  other arithmetic  58.3 us (1%)
    reduce_scatter x1, waiting for transfers between devices, per_device(): lax.psum_scatter(grad_down_w, ('seq', 'head'), scatter_dimension=0, tiled...  1410 us
    reduce_scatter x1, waiting for transfers between devices, per_device(): lax.psum_scatter(grad_up_w, ('seq', 'head'), scatter_dimension=0, tiled=T...  1410 us
    reduce_scatter x1, waiting for transfers between devices, per_device(): lax.psum_scatter(grad_qkv_w, ('seq', 'head'), scatter_dimension=0, tiled=...  440 us
    reduce_scatter x1, waiting for transfers between devices, per_device(): lax.psum_scatter(grad_out_w, ('seq', 'head'), scatter_dimension=0, tiled=...  356 us
    ppermute x8, waiting for transfers between devices, from_behind_2(): lax.ppermute(shard, axis, [(i, (i + by) % length) for i in range(length)])  336 us
    all_gather x1, waiting for transfers between devices, per_device(): lax.all_gather(w_qkv.astype(jnp.bfloat16), ('seq', 'head'), axis=0, tiled...  111 us
  transfers between devices with their start and end apart: 28, of which 14 were waited for; matrix products, arithmetic and copies ran while one was open for 7% of the time, Pallas kernels for 0%

commit v1 on v0

--- a/solution.py
+++ b/solution.py
@@ -3,6 +3,8 @@
 import jax
 import jax.numpy as jnp
 from jax import lax
+from jax.experimental import pallas as pl
+from jax.experimental.pallas import tpu as pltpu
 from jax.sharding import PartitionSpec as P
 
 D = 2048
@@ -120,7 +122,7 @@
     return (grad_query, grad_kv)
 
 
-def per_device(
+def gathered_step(
     inputs,
     doc_lengths,
     ln_gain,
@@ -385,9 +387,474 @@
     )
 
 
+BF = jnp.bfloat16
+F32 = jnp.float32
+AXES = ("seq", "head")
+FF = 8192
+BLOCK = 256
+
+
+def suits(mesh):
+    return mesh.shape["seq"] * mesh.shape["head"] == H and mesh.shape["head"] == 4
+
+
+def coordinates(rank):
+    return rank // 8, (rank // 4) % 2, (rank // 2) % 2, rank % 2
+
+
+def rank_of(z, core, y, x):
+    return ((z * 2 + core) * 2 + y) * 2 + x
+
+
+def route(step):
+    return [(rank, rank_of(*step(*coordinates(rank)))) for rank in range(H)]
+
+
+def ring_place(z, y, length):
+    return z if y == 0 else length - 1 - z
+
+
+def ring_point(place, length):
+    place = place % length
+    return (place, 0) if place < length // 2 else (length - 1 - place, 1)
+
+
+def ring_route(by):
+    length = H // 4
+
+    def step(z, core, y, x):
+        new_z, new_y = ring_point(ring_place(z, y, length) + by, length)
+        return new_z, core, new_y, x
+
+    return route(step)
+
+
+def across_pair(value):
+    return lax.ppermute(value, AXES, route(lambda z, core, y, x: (z, core, y, 1 - x)))
+
+
+def across_cores(value):
+    return lax.ppermute(value, AXES, route(lambda z, core, y, x: (z, 1 - core, y, x)))
+
+
+def up_ring(value):
+    return lax.ppermute(value, AXES, ring_route(1))
+
+
+def down_ring(value):
+    return lax.ppermute(value, AXES, ring_route(-1))
+
+
+def block_index(place, core):
+    length = H // 4
+    place = place % length
+    z = jnp.where(place < length // 2, place, length - 1 - place)
+    y = (place >= length // 2).astype(jnp.int32)
+    return (z * 2 + core) * 2 + y
+
+
+def gather_tokens(own, place, core):
+    rows, width = own.shape
+    half = rows // 2
+    length = H // 4
+    chunks = [(0, own)]
+    up = down = own
+    for hop in range(1, length // 2):
+        up, down = up_ring(up), down_ring(down)
+        chunks += [(-hop, up), (hop, down)]
+    far = jnp.concatenate([up_ring(up[:half]), down_ring(down[half:])], axis=0)
+    chunks += [(length // 2, far)]
+    whole = jnp.zeros((H // 2, rows, width), own.dtype)
+    for offset, chunk in chunks:
+        other = across_cores(chunk)
+        whole = lax.dynamic_update_slice(whole, chunk[None], (block_index(place + offset, core), 0, 0))
+        whole = lax.dynamic_update_slice(
+            whole, other[None], (block_index(place + offset, 1 - core), 0, 0)
+        )
+    return whole.reshape(H // 2 * rows, width)
+
+
+def scatter_tokens(part, place, core):
+    length = H // 4
+    rows = part.shape[0] // (H // 2)
+    half = rows // 2
+    blocks = part.reshape(length // 2, 2, 2, rows, D)
+    for_other = lax.dynamic_index_in_dim(blocks, 1 - core, 1, keepdims=False)
+    from_other = across_cores(for_other)
+
+    def term(offset):
+        index = block_index(place + offset, core)
+        z, y = index // 4, index % 2
+        mine = lax.dynamic_slice(blocks, (z, core, y, 0, 0), (1, 1, 1, rows, D)).reshape(rows, D)
+        theirs = lax.dynamic_slice(from_other, (z, y, 0, 0), (1, 1, rows, D)).reshape(rows, D)
+        return mine.astype(F32) + theirs.astype(F32)
+
+    far = term(length // 2).astype(BF)
+    pad = jnp.zeros((rows - half, D), F32)
+    up = jnp.concatenate([up_ring(far[:half]).astype(F32), pad], axis=0)
+    down = jnp.concatenate([pad, down_ring(far[half:]).astype(F32)], axis=0)
+    for hop in range(length // 2 - 1, 0, -1):
+        up = up_ring((up + term(hop)).astype(BF)).astype(F32)
+        down = down_ring((down + term(-hop)).astype(BF)).astype(F32)
+    return term(0) + up + down
+
+
+def turn(field, tables, sign):
+    half_rot = ROT // 2
+    first = pltpu.roll(field, 2 * HD - half_rot, 1)
+    second = pltpu.roll(field, half_rot, 1)
+    return field * tables[0] + sign * (second * tables[2] - first * tables[1])
+
+
+def turn_tables(count):
+    half_rot = ROT // 2
+    inverse = jnp.power(10000.0, -2.0 * jnp.arange(half_rot, dtype=F32) / ROT)
+    angles = jnp.arange(count, dtype=jnp.int32).astype(F32)[:, None] * inverse[None, :]
+    cosine, sine = jnp.cos(angles), jnp.sin(angles)
+    none = jnp.zeros_like(sine)
+    rest_one, rest_none = jnp.ones((count, HD - ROT), F32), jnp.zeros((count, HD - ROT), F32)
+    one = [
+        jnp.concatenate([cosine, cosine, rest_one], axis=1),
+        jnp.concatenate([sine, none, rest_none], axis=1),
+        jnp.concatenate([none, sine, rest_none], axis=1),
+    ]
+    return jnp.stack([jnp.concatenate([t, t], axis=1) for t in one])
+
+
+def head_lanes(value, head):
+    lane = lax.broadcasted_iota(jnp.int32, value.shape, 1)
+    return jnp.where((lane >= HD) if head else (lane < HD), value, jnp.zeros_like(value))
+
+
+def dot_of(left, right, left_dim, right_dim):
+    return lax.dot_general(
+        left, right, (((left_dim,), (right_dim,)), ((), ())), preferred_element_type=F32
+    )
+
+
+def allowed_keys(starts, key_count, query_first):
+    keys = lax.broadcasted_iota(jnp.int32, (key_count, BLOCK), 0)
+    queries = query_first + lax.broadcasted_iota(jnp.int32, (1, BLOCK), 1)
+    return (keys >= starts) & (keys <= queries)
+
+
+def attend_forward(qkv_ref, bias_ref, tables_ref, starts_ref, q_ref, k_out, v_out, o_ref, low_ref, lse_ref, k_ref, v_ref):
+    step = pl.program_id(0)
+    width = 2 * HD
+    raw = qkv_ref[...] + bias_ref[...]
+    tables = tables_ref[...]
+    here = pl.ds(pl.multiple_of(step * BLOCK, BLOCK), BLOCK)
+    q_ref[...] = turn(raw[:, :width], tables, 1.0).astype(BF)
+    k_ref[here, :] = turn(raw[:, width : 2 * width], tables, 1.0).astype(BF)
+    v_ref[here, :] = raw[:, 2 * width :].astype(BF)
+    k_out[...] = k_ref[here, :]
+    v_out[...] = v_ref[here, :]
+
+    def work(block):
+        count = (block + 1) * BLOCK
+        query = q_ref[...]
+        key, value = k_ref[:count, :], v_ref[:count, :]
+        allowed = allowed_keys(starts_ref[...], count, block * BLOCK)
+        outs, logs = [], []
+        for head in range(2):
+            scores = dot_of(key, head_lanes(query, head), 1, 1) * 0.125
+            scores = jnp.where(allowed, scores, NEG_FILL)
+            top = jnp.max(scores, axis=0, keepdims=True)
+            weights = jnp.exp(scores - top)
+            total = jnp.sum(weights, axis=0, keepdims=True)
+            outs.append(dot_of(value, weights.astype(BF), 0, 0) / total)
+            logs.append(top + jnp.log(total))
+        row = lax.broadcasted_iota(jnp.int32, outs[0].shape, 0)
+        out = jnp.where(row < HD, outs[0], outs[1]).T
+        o_ref[...] = out
+        low_ref[...] = out.astype(BF)
+        lse_ref[...] = jnp.concatenate(logs, axis=0)
+
+    for block in range(pl.num_programs(0)):
+        pl.when(step == block)(partial(work, block))
+
+
+def attend_backward(q_ref, k_ref, v_ref, g_ref, o_ref, lse_ref, tables_ref, starts_ref, out_ref, gk_ref, gv_ref):
+    step = pl.program_id(0)
+    steps = pl.num_programs(0)
+    width = 2 * HD
+
+    @pl.when(step == 0)
+    def _():
+        gk_ref[...] = jnp.zeros_like(gk_ref)
+        gv_ref[...] = jnp.zeros_like(gv_ref)
+
+    def work(block):
+        count = (block + 1) * BLOCK
+        query, grad = q_ref[...], g_ref[...]
+        key, value = k_ref[:count, :], v_ref[:count, :]
+        allowed = allowed_keys(starts_ref[...], count, block * BLOCK)
+        product = (grad.astype(F32) * o_ref[...]).T
+        grad_q = None
+        for head in range(2):
+            dots = jnp.sum(product[head * HD : (head + 1) * HD], axis=0, keepdims=True)
+            query_h, grad_h = head_lanes(query, head), head_lanes(grad, head)
+            scores = dot_of(key, query_h, 1, 1) * 0.125
+            probs = jnp.where(allowed, jnp.exp(scores - lse_ref[head : head + 1, :]), 0.0)
+            grad_probs = dot_of(value, grad_h, 1, 1)
+            grad_scores = (probs * (grad_probs - dots)).astype(BF)
+            gv_ref[:count, :] += dot_of(probs.astype(BF), grad_h, 1, 0)
+            gk_ref[:count, :] += dot_of(grad_scores, query_h, 1, 0)
+            this = dot_of(head_lanes(key, head), grad_scores, 0, 0)
+            grad_q = this if grad_q is None else grad_q + this
+        here = slice(block * BLOCK, count)
+        tables = tables_ref[...]
+
+        def back(value):
+            return turn((value * 0.125).astype(BF).astype(F32), tables, -1.0).astype(BF)
+
+        out_ref[:, :width] = back(grad_q.T)
+        out_ref[:, width : 2 * width] = back(gk_ref[here, :])
+        out_ref[:, 2 * width :] = gv_ref[here, :].astype(BF)
+
+    for block in range(steps):
+        pl.when(step == steps - 1 - block)(partial(work, block))
+
+
+def attention_forward(qkv, bias, tables, starts):
+    count = qkv.shape[0]
+    width = 2 * HD
+    steps = count // BLOCK
+    rows = lambda i: (i, 0)
+    block = pl.BlockSpec((BLOCK, width), rows)
+    return pl.pallas_call(
+        attend_forward,
+        grid=(steps,),
+        in_specs=[
+            pl.BlockSpec((BLOCK, 3 * width), rows),
+            pl.BlockSpec((1, 3 * width), lambda i: (0, 0)),
+            pl.BlockSpec((3, BLOCK, width), lambda i: (0, i, 0)),
+            pl.BlockSpec((1, BLOCK), lambda i: (0, i)),
+        ],
+        out_specs=[block] * 5 + [pl.BlockSpec((2, BLOCK), lambda i: (0, i))],
+        out_shape=[
+            jax.ShapeDtypeStruct((count, width), BF),
+            jax.ShapeDtypeStruct((count, width), BF),
+            jax.ShapeDtypeStruct((count, width), BF),
+            jax.ShapeDtypeStruct((count, width), F32),
+            jax.ShapeDtypeStruct((count, width), BF),
+            jax.ShapeDtypeStruct((2, count), F32),
+        ],
+        scratch_shapes=[pltpu.VMEM((count, width), BF), pltpu.VMEM((count, width), BF)],
+        cost_estimate=pl.CostEstimate(
+            flops=8 * count * count * HD, bytes_accessed=8 * count * width * 2, transcendentals=count * count
+        ),
+        name="attend_forward",
+    )(qkv, bias, tables, starts)
+
+
+def attention_backward(query, key, value, grad, out, logs, tables, starts):
+    count = query.shape[0]
+    width = 2 * HD
+    steps = count // BLOCK
+    rows = lambda i: (steps - 1 - i, 0)
+    block = pl.BlockSpec((BLOCK, width), rows)
+    full = pl.BlockSpec((count, width), lambda i: (0, 0))
+    return pl.pallas_call(
+        attend_backward,
+        grid=(steps,),
+        in_specs=[
+            block,
+            full,
+            full,
+            block,
+            block,
+            pl.BlockSpec((2, BLOCK), lambda i: (0, steps - 1 - i)),
+            pl.BlockSpec((3, BLOCK, width), lambda i: (0, steps - 1 - i, 0)),
+            pl.BlockSpec((1, BLOCK), lambda i: (0, steps - 1 - i)),
+        ],
+        out_specs=pl.BlockSpec((BLOCK, 3 * width), rows),
+        out_shape=jax.ShapeDtypeStruct((count, 3 * width), BF),
+        scratch_shapes=[pltpu.VMEM((count, width), F32), pltpu.VMEM((count, width), F32)],
+        cost_estimate=pl.CostEstimate(
+            flops=20 * count * count * HD, bytes_accessed=8 * count * width * 2, transcendentals=count * count
+        ),
+        name="attend_backward",
+    )(query, key, value, grad, out, logs, tables, starts)
+
+
+def normalize(values):
+    center = values - jnp.mean(values, axis=-1, keepdims=True)
+    scale = lax.rsqrt(jnp.mean(center * center, axis=-1, keepdims=True) + 1e-05)
+    return center * scale, scale
+
+
+def paired_step(
+    inputs,
+    doc_lengths,
+    ln_gain,
+    ln_bias,
+    w_qkv,
+    b_qkv,
+    w_out,
+    b_out,
+    w_fc1,
+    b_fc1,
+    w_fc2,
+    b_fc2,
+    cotangent,
+):
+    rows = inputs.shape[1]
+    count = rows * H
+    rank = lax.axis_index("seq") * 4 + lax.axis_index("head")
+    x = rank % 2
+    y, core, z = (rank // 2) % 2, (rank // 4) % 2, rank // 8
+    length = H // 4
+    place = jnp.where(y == 0, z, length - 1 - z)
+    doc_ends = jnp.cumsum(lax.dynamic_index_in_dim(doc_lengths, x, 0, keepdims=False))
+    positions = jnp.arange(count, dtype=jnp.int32)
+    starts = jnp.max(
+        jnp.where(doc_ends[:, None] <= positions[None, :], doc_ends[:, None], 0), axis=0
+    )[None, :]
+    tables = turn_tables(count)
+
+    def to_group(field):
+        mine = lax.dynamic_index_in_dim(field, x, 0, keepdims=False)
+        got = across_pair(lax.dynamic_index_in_dim(field, 1 - x, 0, keepdims=False))
+        return jnp.where(x == 0, jnp.concatenate([mine, got]), jnp.concatenate([got, mine]))
+
+    def from_group(field):
+        mine = lax.dynamic_slice_in_dim(field, x * rows, rows, 0)
+        got = across_pair(lax.dynamic_slice_in_dim(field, (1 - x) * rows, rows, 0))
+        return jnp.where(x == 0, jnp.stack([mine, got]), jnp.stack([got, mine]))
+
+    own_in = to_group(inputs)
+    all_in = gather_tokens(own_in, place, core)
+    small = jnp.concatenate([ln_gain, ln_bias, b_out, b_fc2, b_qkv, b_fc1]).astype(BF)
+    small = lax.all_gather(small[None], AXES, axis=0, tiled=True).astype(F32)
+    per = D // H
+    gain, shift, out_bias, down_bias = [
+        small[:, i * per : (i + 1) * per].reshape(1, D) for i in range(4)
+    ]
+    qkv_bias_all = small[:, 4 * per : 4 * per + 3 * per].reshape(3, H, HD)
+    up_bias_all = small[:, 7 * per :]
+    other = rank + 1 - 2 * x
+
+    def both(table, axis):
+        return [lax.dynamic_index_in_dim(table, i, axis, keepdims=False) for i in (rank, other)]
+
+    qkv_bias = jnp.concatenate(both(qkv_bias_all, 1), axis=1).reshape(1, 6 * HD)
+    up_bias = jnp.concatenate(both(up_bias_all, 0), axis=0)[None, :]
+
+    per_ff = FF // H
+    to_heads = jnp.concatenate(
+        [
+            w_qkv.astype(BF).reshape(per, 3, H, HD).transpose(2, 0, 1, 3).reshape(H, per, 3 * HD),
+            w_fc1.astype(BF).reshape(per, H, per_ff).transpose(1, 0, 2),
+        ],
+        axis=2,
+    )
+    mine_w = lax.all_to_all(to_heads, AXES, 0, 0, tiled=True).reshape(D, 3 * HD + per_ff)
+    pair_w = across_pair(mine_w)
+    qkv_w = jnp.stack(
+        [mine_w[:, : 3 * HD].reshape(D, 3, HD), pair_w[:, : 3 * HD].reshape(D, 3, HD)], axis=2
+    ).reshape(D, 6 * HD)
+    up_w = jnp.concatenate([mine_w[:, 3 * HD :], pair_w[:, 3 * HD :]], axis=1)
+    mine_d = jnp.concatenate([w_out, w_fc2], axis=0).astype(BF)
+    pair_d = across_pair(mine_d)
+    down_w = jnp.concatenate([mine_d[:per], pair_d[:per], mine_d[per:], pair_d[per:]], axis=0)
+
+    normed = (normalize(all_in.astype(F32))[0] * gain + shift).astype(BF)
+    qkv = jnp.dot(normed, qkv_w, preferred_element_type=F32)
+    query, key, value, out_full, attended, logs = attention_forward(qkv, qkv_bias, tables, starts)
+    hidden = jnp.dot(normed, up_w, preferred_element_type=F32) + up_bias
+    active, gelu_back = jax.vjp(gelu_tanh, hidden)
+    mixed = jnp.concatenate([attended, active.astype(BF)], axis=1)
+    forward_part = jnp.dot(mixed, down_w, preferred_element_type=F32).astype(BF)
+    forward_sum = scatter_tokens(forward_part, place, core)
+    output = from_group(
+        (own_in.astype(F32) + (forward_sum + (out_bias + down_bias))).astype(BF)
+    )
+
+    own_cot = to_group(cotangent)
+    all_cot = gather_tokens(own_cot, place, core)
+    grad_mixed = dot_of(all_cot, down_w, 1, 1)
+    grad_att = grad_mixed[:, : 2 * HD].astype(BF)
+    grad_hidden = gelu_back(grad_mixed[:, 2 * HD :])[0].astype(BF)
+    grad_down = dot_of(mixed, all_cot, 0, 0)
+    grad_qkv = attention_backward(query, key, value, grad_att, out_full, logs, tables, starts)
+    grad_qkv_w = dot_of(normed, grad_qkv, 0, 0)
+    grad_up_w = dot_of(normed, grad_hidden, 0, 0)
+    back_part = dot_of(grad_qkv, qkv_w, 1, 1) + dot_of(grad_hidden, up_w, 1, 1)
+    normal_all = normalize(all_in.astype(F32))[0]
+    grad_gain = jnp.sum(back_part * normal_all, axis=0)
+    grad_shift = jnp.sum(back_part, axis=0)
+    back_sum = scatter_tokens(back_part.astype(BF), place, core)
+    normal, scale = normalize(own_in.astype(F32))
+    scaled = back_sum * gain
+    grad_in = scale * (
+        scaled
+        - jnp.mean(scaled, axis=-1, keepdims=True)
+        - normal * jnp.mean(scaled * normal, axis=-1, keepdims=True)
+    )
+    grad_input = from_group((own_cot.astype(F32) + grad_in).astype(BF))
+
+    def add_pair(mine, for_pair):
+        return mine + across_pair(for_pair.astype(BF)).astype(F32)
+
+    grad_out_rows = add_pair(grad_down[:per], grad_down[per : 2 * per])
+    grad_down_rows = add_pair(
+        grad_down[2 * per : 2 * per + per_ff], grad_down[2 * per + per_ff :]
+    )
+    grad_heads = grad_qkv_w.reshape(D, 3, 2, HD)
+    grad_cols = jnp.concatenate(
+        [
+            add_pair(grad_heads[:, :, 0], grad_heads[:, :, 1]).reshape(D, 3 * HD),
+            add_pair(grad_up_w[:, :per_ff], grad_up_w[:, per_ff:]),
+        ],
+        axis=1,
+    ).astype(BF)
+    grad_rows = lax.all_to_all(
+        grad_cols.reshape(H, per, 3 * HD + per_ff), AXES, 0, 0, tiled=True
+    ).astype(F32)
+    grad_qkv_rows = (
+        grad_rows[:, :, : 3 * HD].reshape(H, per, 3, HD).transpose(1, 2, 0, 3).reshape(per, 3 * D)
+    )
+    grad_up_rows = grad_rows[:, :, 3 * HD :].transpose(1, 0, 2).reshape(per, FF)
+
+    cot_sum = jnp.sum(own_cot.astype(F32), axis=0)
+    head_sums = jnp.sum(grad_qkv.astype(F32), axis=0).reshape(3, 2, HD)
+    up_sums = jnp.sum(grad_hidden.astype(F32), axis=0).reshape(2, per_ff)
+    qkv_sums = jnp.zeros((3, H, HD), F32)
+    up_all = jnp.zeros((H, per_ff), F32)
+    for which, index in enumerate((rank, other)):
+        qkv_sums = lax.dynamic_update_slice(qkv_sums, head_sums[:, which : which + 1], (0, index, 0))
+        up_all = lax.dynamic_update_slice(up_all, up_sums[which : which + 1], (index, 0))
+    sums = jnp.concatenate(
+        [
+            grad_gain.reshape(H, per),
+            grad_shift.reshape(H, per),
+            cot_sum.reshape(H, per),
+            qkv_sums.reshape(H, 3 * per),
+            up_all,
+        ],
+        axis=1,
+    )
+    sums = lax.psum_scatter(sums, AXES, scatter_dimension=0, tiled=True).reshape(-1)
+    return (
+        output,
+        grad_input,
+        sums[:per],
+        sums[per : 2 * per],
+        grad_qkv_rows,
+        sums[3 * per : 6 * per],
+        grad_out_rows,
+        sums[2 * per : 3 * per],
+        grad_up_rows,
+        sums[6 * per :],
+        grad_down_rows,
+        sums[2 * per : 3 * per],
+    )
+
+
 def solution(mesh):
     return jax.shard_map(
-        per_device,
+        paired_step if suits(mesh) else gathered_step,
         mesh=mesh,
         in_specs=(
             P(None, ("seq", "head"), None),

time: 4810 us -> 793 us (0.16)
  waiting for transfers between devices: 4100 us -> 231 us
  matrix products: 195 us -> 87.4 us
  starting transfers between devices: 162 us -> 75 us
    reduce_scatter x4 -> x0, waiting for transfers between devices: 3610 us -> none  [the longest x1 1410 us: per_device(): lax.psum_scatter(grad_down_w, ('seq', 'head'), scatter_dimension=0, tiled...]
    ppermute x15 -> x60, waiting for transfers between devices: 336 us -> 136 us  [the longest x16 72.8 us: up_ring(): return lax.ppermute(value, AXES, ring_route(1))]
    all_gather x5 -> x0, waiting for transfers between devices: 111 us -> none  [the longest x1 111 us: per_device(): lax.all_gather(w_qkv.astype(jnp.bfloat16), ('seq', 'head'), axis=0, tiled...]
    dot_general x26 -> x9, matrix products: 195 us -> 87.4 us  [the longest x6 58.3 us: dot_of(): lax.dot_general(left, right, (((left_dim,), (right_dim,)), ((), ())), pre...]
    ppermute x15 -> x60, starting transfers between devices: 139 us -> 64.5 us  [the longest x16 35.5 us: up_ring(): return lax.ppermute(value, AXES, ring_route(1))]
    unnamed x11 -> x2, waiting for transfers between devices: 42.7 us -> 94.9 us
  transfers between devices with their start and end apart: 28 -> 63, of which waited for: 14 -> 21; matrix products, arithmetic and copies ran while one was open for 7% -> 32% of each run, Pallas kernels for 0% -> 0%
where the time goes in v1:
time: 793 us; the launch traced here: 778 us
  waiting for transfers between devices  231 us (29%)
  local copies, waits for them, and re-layouts  126 us (16%)
  blocking collectives  109 us (14%)
  matrix products  87.4 us (11%)
  other arithmetic  87.2 us (11%)
  starting transfers between devices  75 us (9%)
  Pallas kernels  46.8 us (6%)
  between operations  16.3 us (2%)
    all_gather x1, blocking collectives, paired_step(): small = lax.all_gather(small[None], AXES, axis=0, tiled=True).astype(F32)  109 us
    unnamed x2, waiting for transfers between devices  94.9 us
    ppermute x16, waiting for transfers between devices, up_ring(): return lax.ppermute(value, AXES, ring_route(1))  72.8 us
    dot_general x6, matrix products, dot_of(): lax.dot_general(left, right, (((left_dim,), (right_dim,)), ((), ())), pre...  58.3 us
    ppermute x16, waiting for transfers between devices, down_ring(): return lax.ppermute(value, AXES, ring_route(-1))  40.8 us
    ppermute x16, starting transfers between devices, up_ring(): return lax.ppermute(value, AXES, ring_route(1))  35.5 us
    pallas_call x1, Pallas kernels, attention_forward(): pl.pallas_call(attend_forward, grid=(steps,), in_specs=[pl.BlockSpec((BLO...  27.5 us
    unnamed x91, local copies, waits for them, and re-layouts  22.1 us
  transfers between devices with their start and end apart: 63, of which 21 were waited for; matrix products, arithmetic and copies ran while one was open for 32% of the time, Pallas kernels for 0%

profile of v1, /device:TPU:0, one launch (start us, length us, event | category | flops | bytes accessed | tf_op | source)
XLA Modules:
  0.0 778.5 jit_solution(5636628280912519248)
XLA Ops:
  23.5 6.5 all-to-all-start
  35.5 109.5 %all-gather = bf16[32,1,704]{2,1,0:T(2,128)(2,1)S(1)} all-gather(bf16[1,1,704]{2,1,0:T(2,128)(2,1)S(1)} %bitcast.322), channel_id=1, replica_groups=mesh['seq'=8,'head'=4] {'seq','head'}, dimensions={0}, use_global_device_ids=true | all-gather | bytes 46464 | tf_op jit(solution)/shard_map/all_gather | solution.py:729
  194.8 10.5 %collective-permute-done.4 = bf16[128,2048]{1,0:T(8,128)(2,1)S(1)} collective-permute-done((bf16[128,2048]{1,0:T(8,128)(2,1)S(1)}, bf16[128,2048]{1,0:T(8,128)(2,1)S(1)}, u32[]{:S(2)}, u32[]{:S(2)}) %collective-permute-start.4) | collective-permute-done | bytes 524320 | tf_op jit(solution)/shard_map/ppermute | solution.py:445
  211.6 10.6 %collective-permute-done.6 = bf16[128,2048]{1,0:T(8,128)(2,1)S(1)} collective-permute-done((bf16[128,2048]{1,0:T(8,128)(2,1)S(1)}, bf16[128,2048]{1,0:T(8,128)(2,1)S(1)}, u32[]{:S(2)}, u32[]{:S(2)}) %collective-permute-start.6) | collective-permute-done | bytes 524320 | tf_op jit(solution)/shard_map/ppermute | solution.py:441
  224.4 8.1 %collective-permute-done.35 = bf16[128,2048]{1,0:T(8,128)(2,1)S(1)} collective-permute-done((bf16[128,2048]{1,0:T(8,128)(2,1)S(1)}, bf16[128,2048]{1,0:T(8,128)(2,1)S(1)}, u32[]{:S(2)}, u32[]{:S(2)}) %collective-permute-start.35) | collective-permute-done | bytes 524320 | tf_op jit(solution)/shard_map/ppermute | solution.py:441
  243.2 10.2 %collective-permute-done.41 = bf16[128,2048]{1,0:T(8,128)(2,1)S(1)} collective-permute-done((bf16[128,2048]{1,0:T(8,128)(2,1)S(1)}, bf16[128,2048]{1,0:T(8,128)(2,1)S(1)}, u32[]{:S(2)}, u32[]{:S(2)}) %collective-permute-start.41) | collective-permute-done | bytes 524320 | tf_op jit(solution)/shard_map/ppermute | solution.py:445
  255.2 9.4 %collective-permute-done.12 = bf16[128,2048]{1,0:T(8,128)(2,1)S(1)} collective-permute-done((bf16[128,2048]{1,0:T(8,128)(2,1)S(1)}, bf16[128,2048]{1,0:T(8,128)(2,1)S(1)}, u32[]{:S(2)}, u32[]{:S(2)}) %collective-permute-start.12) | collective-permute-done | bytes 524320 | tf_op jit(solution)/shard_map/ppermute | solution.py:445
  286.9 9.2 %fusion.58 = f32[2048,640]{1,0:T(8,128)S(1)} fusion(bf16[2048,2048]{1,0:T(8,128)(2,1)} %bitcast.79, bf16[256,2048]{1,0:T(8,128)(2,1)S(1)} %slice.217, bf16[256,2048]{1,0:T(8,128)(2,1)S(1)} %copy-done.7, bf16[64,2048]{1,0:T(8,128)(2,1)S(1)} %slice.216, bf16[64,2048]{1,0:T(8,128)(2,1)S(1)} %copy-done.17), kind=kOutput, calls=%fused_computation.148 | convolution fusion | flops 5379194880 | bytes 16252928 | tf_op jit(solution)/shard_map/dot_general | solution.py:530
  313.5 8.7 %add_convert_fusion.1 = bf16[16,128,2048]{2,1,0:T(8,128)(2,1)} fusion(bf16[16,128,2048]{2,1,0:T(8,128)(2,1)} %bitcast_dynamic-update-slice_fusion.15, f32[2048]{0:T(1024)S(1)} %add.826, f32[2048]{0:T(1024)S(1)} %mul.365, f32[16,128]{1,0:T(8,128)S(1)} %get-tuple-element.123, f32[16,128]{1,0:T(8,128)S(1)} %get-tuple-element.126), kind=kLoop, calls=%fused_computation.4 | loop fusion | flops 25165824 | bytes 16809984 | tf_op jit(solution)/shard_map/convert_element_type | solution.py:762
  322.2 8.6 %add_convert_fusion = bf16[2048,2048]{1,0:T(8,128)(2,1)} fusion(bf16[16,128,2048]{2,1,0:T(8,128)(2,1)} %bitcast_dynamic-update-slice_fusion.15, f32[2048]{0:T(1024)S(1)} %add.826, f32[2048]{0:T(1024)S(1)} %mul.365, f32[2048]{0:T(1024)S(1)} %get-tuple-element.124, f32[2048]{0:T(1024)S(1)} %get-tuple-element.125), kind=kLoop, calls=%fused_computation.3 | loop fusion | flops 25165824 | bytes 16809984 | tf_op jit(solution)/shard_map/convert_element_type | solution.py:762
  335.4 20.8 %collective-permute-done.17 = bf16[2048,448]{0,1:T(8,128)(2,1)} collective-permute-done((bf16[2048,448]{0,1:T(8,128)(2,1)}, bf16[2048,448]{0,1:T(8,128)(2,1)}, u32[]{:S(2)}, u32[]{:S(2)}) %collective-permute-start.17) | collective-permute-done | bytes 1835040 | tf_op jit(solution)/shard_map/ppermute | solution.py:433
  357.6 8.7 %fusion.76.qkv_ref = f32[2048,384]{1,0:T(8,128)} fusion(bf16[2048,2048]{1,0:T(8,128)(2,1)} %bitcast.302, bf16[2048,384]{0,1:T(8,128)(2,1)S(1)} %bitcast.304), kind=kOutput, calls=%fused_computation.205 | convolution fusion | flops 3221225472 | bytes 13107200 | tf_op jit(solution)/shard_map/dot_general | solution.py:763
  366.3 27.5 %attend_forward.1 = (bf16[2048,128]{1,0:T(8,128)(2,1)}, bf16[2048,128]{1,0:T(8,128)(2,1)}, bf16[2048,128]{1,0:T(8,128)(2,1)}, f32[2048,128]{1,0:T(8,128)}, bf16[2048,128]{1,0:T(8,128)(2,1)}, /*index=5*/f32[2,2048]{1,0:T(2,128)}) custom-call(f32[2048,384]{1,0:T(8,128)} %fusion.76.qkv_ref, f32[1,384]{1,0:T(1,128)} %bitcast.331, ...), custom_call_target="tpu_custom_call" | custom-call | flops 2147483648 | bytes 4194304 | tf_op jit(solution)/shard_map/attend_forward/pallas_call | solution.py:625
  393.8 19.3 %attend_backward.1 = bf16[2048,384]{1,0:T(8,128)(2,1)} custom-call(bf16[2048,128]{1,0:T(8,128)(2,1)} %get-tuple-element.19.q_ref, bf16[2048,128]{1,0:T(8,128)(2,1)} %get-tuple-element.20.k_ref, bf16[2048,128]{1,0:T(8,128)(2,1)} %get-tuple-element.21.v_ref, bf16[2048,128]{1,0:T(8,128)(2,1)} %slice.259.g_ref, f32[2048,128]{1,0:T(8,128)} %get-tuple-element.22.o_ref, ...), custom_call_target="tpu_custom_call" | custom-call | flops 5368709120 | bytes 4194304 | tf_op jit(solution)/shard_map/attend_backward/pallas_call | solution.py:658
  414.8 9.5 %fusion.77 = f32[2048,2048]{1,0:T(8,128)} fusion(bf16[2048,384]{1,0:T(8,128)(2,1)} %attend_backward.1, bf16[2048,384]{0,1:T(8,128)(2,1)S(1)} %bitcast.305), kind=kOutput, calls=%fused_computation.206 | convolution fusion | flops 3221225472 | bytes 19922944 | tf_op jit(solution)/shard_map/dot_general | solution.py:530
  439.4 13.2 %convert_reduce_fusion.1 = (f32[512]{0:T(512)S(1)}, bf16[2048,512]{1,0:T(8,128)(2,1)}, bf16[2048,512]{1,0:T(8,128)(2,1)}) fusion(f32[512]{0:T(512)S(1)} %pad_maximum_fusion.14, f32[2048,640]{1,0:T(8,128)} %copy-done.25, bf16[2048,2048]{1,0:T(8,128)(2,1)} %add_convert_fusion, bf16[2048,256]{1,0:T(8,128)(2,1)S(1)} %copy-done.22, ...), kind=kOutput, calls=%fused_computation.18 | convolution fusion | flops 4325375488 | bytes 18878464 | tf_op jit(solution)/shard_map/dot_general | solution.py:765
  452.6 14.2 %fusion.67 = (f32[2048]{0:T(1024)S(1)}, f32[2048]{0:T(1024)S(1)}, bf16[2048,2048]{1,0:T(8,128)(2,1)}) fusion(f32[2048]{0:T(1024)S(1)} %get-tuple-element.124, f32[2048]{0:T(1024)S(1)} %get-tuple-element.125, bf16[16,128,2048]{2,1,0:T(8,128)(2,1)} %bitcast_dynamic-update-slice_fusion.15, f32[2048,2048]{1,0:T(8,128)} %fusion.77, ...), kind=kOutput, calls=%fused_computation.198 | convolution fusion | flops 4332711936 | bytes 37781504 | tf_op jit(solution)/shard_map/dot_general | solution.py:530
  471.9 7.3 convolution_convert_fusion
  486.6 7.7 fusion.79
  494.4 11.2 %fusion.75 = (bf16[640,2048]{1,0:T(8,128)(2,1)S(1)}, f32[640,2048]{1,0:T(8,128)}) fusion(bf16[2048,2048]{1,0:T(8,128)(2,1)} %bitcast.79, bf16[2048,512]{1,0:T(8,128)(2,1)S(1)} %copy-done.39, bf16[2048,128]{1,0:T(8,128)(2,1)S(1)} %copy-done.37), kind=kOutput, calls=%fused_computation.204 | convolution fusion | flops 5375262720 | bytes 18874368 | tf_op jit(solution)/shard_map/dot_general | solution.py:530
  510.5 94.9 %all-reduce.7.cloned.1.call-done = f32[32,640]{1,0:T(8,128)} async-done(((f32[32,640]{1,0:T(8,128)}), f32[32,640]{1,0:T(8,128)}) %all-reduce.7.cloned.1.call-update) | async-done | bytes 81936
  664.2 8.8 %collective-permute-done.49 = bf16[128,2048]{1,0:T(8,128)(2,1)} collective-permute-done((bf16[128,2048]{1,0:T(8,128)(2,1)}, bf16[128,2048]{1,0:T(8,128)(2,1)}, u32[]{:S(2)}, u32[]{:S(2)}) %collective-permute-start.49) | collective-permute-done | bytes 524320 | tf_op jit(solution)/shard_map/ppermute | solution.py:441
  684.5 26.4 %collective-permute-done.22 = bf16[128,2048]{1,0:T(8,128)(2,1)S(1)} collective-permute-done((bf16[128,2048]{1,0:T(8,128)(2,1)S(1)}, bf16[128,2048]{1,0:T(8,128)(2,1)S(1)}, u32[]{:S(2)}, u32[]{:S(2)}) %collective-permute-start.22) | collective-permute-done | bytes 524320 | tf_op jit(solution)/shard_map/ppermute | solution.py:441
  714.6 15.1 %collective-permute-start.23 = (bf16[128,2048]{1,0:T(8,128)(2,1)S(1)}, bf16[128,2048]{1,0:T(8,128)(2,1)S(1)}, u32[]{:S(2)}, u32[]{:S(2)}) collective-permute-start(bf16[128,2048]{1,0:T(8,128)(2,1)S(1)} %get-tuple-element.90), channel_id=1, source_target_pairs={{0,8},{1,9},{2,0},{3,1},{4,12},{5,13},{6,4},{7,5},{8,16},{9,17},{1... | collective-permute-start | bytes 1572872 | tf_op jit(solution)/shard_map/ppermute | solution.py:441
  (367 shorter events, 286.4 us)
Async XLA Ops:
  9.0 163.0 %collective-permute-start = (bf16[64,2048]{1,0:T(8,128)(2,1)}, bf16[64,2048]{1,0:T(8,128)(2,1)}, u32[]{:S(2)}, u32[]{:S(2)}) collective-permute-start(bf16[64,2048]{1,0:T(8,128)(2,1)} %get-tuple-element.109), channel_id=1, source_target_pairs={{0,1},{1,0},{2,3},{3,2},{4,5},{5,4},{6,7},{7,6},{8,9},{9,8},{10,11... | collective-permute-start | bytes 786440 | tf_op jit(solution)/shard_map/ppermute | solution.py:433
  13.8 154.9 %collective-permute-start.29 = (bf16[64,2048]{1,0:T(8,128)(2,1)}, bf16[64,2048]{1,0:T(8,128)(2,1)}, u32[]{:S(2)}, u32[]{:S(2)}) collective-permute-start(bf16[64,2048]{1,0:T(8,128)(2,1)} %get-tuple-element.103), channel_id=1, source_target_pairs={{0,1},{1,0},{2,3},{3,2},{4,5},{5,4},{6,7},{7,6},{8,9},{9,8},{10,11... | collective-permute-start | bytes 786440 | tf_op jit(solution)/shard_map/ppermute | solution.py:433
  23.5 286.1 %all-to-all-start = ((bf16[32,64,448]{2,1,0:T(8,128)(2,1)}), bf16[32,64,448]{2,1,0:T(8,128)(2,1)}, u32[]{:S(2)}, u32[]{:S(2)}) async-start(bf16[32,64,448]{2,1,0:T(8,128)(2,1)} %pad_maximum_fusion.3), calls=%async_computation | async-start | bytes 4194304 | tf_op jit(solution)/shard_map/all_to_all | solution.py:752
  30.0 575.3 %all-reduce.7.cloned.1.call-start = ((), (), s32[]{:S(2)}) async-start(), calls=%async_computation.2 | async-start | bytes 163840
  33.5 201.5 %collective-permute-start.18 = (bf16[320,2048]{1,0:T(8,128)(2,1)}, bf16[320,2048]{1,0:T(8,128)(2,1)}, u32[]{:S(2)}, u32[]{:S(2)}) collective-permute-start(bf16[320,2048]{1,0:T(8,128)(2,1)} %pad_maximum_fusion.11), channel_id=1, source_target_pairs={{0,1},{1,0},{2,3},{3,2},{4,5},{5,4},{6,7},{7,6},{8,9},{9,8},{10,11... | collective-permute-start | bytes 3932168 | tf_op jit(solution)/shard_map/ppermute | solution.py:433
  192.6 45.7 %collective-permute-start.37 = (bf16[128,2048]{1,0:T(8,128)(2,1)S(1)}, bf16[128,2048]{1,0:T(8,128)(2,1)S(1)}, u32[]{:S(2)}, u32[]{:S(2)}) collective-permute-start(bf16[128,2048]{1,0:T(8,128)(2,1)S(1)} %collective-permute-done.33), channel_id=1, source_target_pairs={{0,2},{1,3},{2,10},{3,11},{4,6},{5,7},{6,14},{7,15},{8,0},{9,1},{1... | collective-permute-start | bytes 1572872 | tf_op jit(solution)/shard_map/ppermute | solution.py:445
  193.6 30.8 %collective-permute-start.34 = (bf16[128,2048]{1,0:T(8,128)(2,1)S(1)}, bf16[128,2048]{1,0:T(8,128)(2,1)S(1)}, u32[]{:S(2)}, u32[]{:S(2)}) collective-permute-start(bf16[128,2048]{1,0:T(8,128)(2,1)S(1)} %collective-permute-done.33), channel_id=1, source_target_pairs={{0,4},{1,5},{2,6},{3,7},{4,0},{5,1},{6,2},{7,3},{8,12},{9,13},{10,... | collective-permute-start | bytes 1572872 | tf_op jit(solution)/shard_map/ppermute | solution.py:437
  238.3 26.3 %collective-permute-start.10 = (bf16[128,2048]{1,0:T(8,128)(2,1)S(1)}, bf16[128,2048]{1,0:T(8,128)(2,1)S(1)}, u32[]{:S(2)}, u32[]{:S(2)}) collective-permute-start(bf16[128,2048]{1,0:T(8,128)(2,1)S(1)} %collective-permute-done.6), channel_id=1, source_target_pairs={{0,8},{1,9},{2,0},{3,1},{4,12},{5,13},{6,4},{7,5},{8,16},{9,17},{1... | collective-permute-start | bytes 1572872 | tf_op jit(solution)/shard_map/ppermute | solution.py:441
  242.3 25.3 %collective-permute-start.9 = (bf16[128,2048]{1,0:T(8,128)(2,1)S(1)}, bf16[128,2048]{1,0:T(8,128)(2,1)S(1)}, u32[]{:S(2)}, u32[]{:S(2)}) collective-permute-start(bf16[128,2048]{1,0:T(8,128)(2,1)S(1)} %collective-permute-done.8), channel_id=1, source_target_pairs={{0,4},{1,5},{2,6},{3,7},{4,0},{5,1},{6,2},{7,3},{8,12},{9,13},{10,... | collective-permute-start | bytes 1572872 | tf_op jit(solution)/shard_map/ppermute | solution.py:437
  313.5 42.6 %collective-permute-start.17 = (bf16[2048,448]{0,1:T(8,128)(2,1)}, bf16[2048,448]{0,1:T(8,128)(2,1)}, u32[]{:S(2)}, u32[]{:S(2)}) collective-permute-start(bf16[2048,448]{0,1:T(8,128)(2,1)} %copy.75), channel_id=1, source_target_pairs={{0,1},{1,0},{2,3},{3,2},{4,5},{5,4},{6,7},{7,6},{8,9},{9,8},{10,11... | collective-permute-start | bytes 5505032 | tf_op jit(solution)/shard_map/ppermute | solution.py:433
  439.1 170.3 %collective-permute-start.56 = (bf16[2048,3,64]{0,2,1:T(8,128)(2,1)S(1)}, bf16[2048,3,64]{0,2,1:T(8,128)(2,1)}, u32[]{:S(2)}, u32[]{:S(2)}) collective-permute-start(bf16[2048,3,64]{0,2,1:T(8,128)(2,1)S(1)} %fusion.55), channel_id=1, source_target_pairs={{0,1},{1,0},{2,3},{3,2},{4,5},{5,4},{6,7},{7,6},{8,9},{9,8},{10,11... | collective-permute-start | bytes 2359304 | tf_op jit(solution)/shard_map/ppermute | solution.py:433
  471.8 142.4 %collective-permute-start.46 = (bf16[4,2,128,2048]{3,2,1,0:T(8,128)(2,1)}, bf16[4,2,128,2048]{3,2,1,0:T(8,128)(2,1)}, u32[]{:S(2)}, u32[]{:S(2)}) collective-permute-start(bf16[4,2,128,2048]{3,2,1,0:T(8,128)(2,1)} %dynamic-slice_bitcast_fusion), channel_id=1, source_target_pairs={{0,4},{1,5},{2,6},{3,7},{4,0},{5,1},{6,2},{7,3},{8,12},{9,13},{10,... | collective-permute-start | bytes 12582920 | tf_op jit(solution)/shard_map/ppermute | solution.py:437
  485.1 135.1 %collective-permute-start.19 = (bf16[4,2,128,2048]{3,2,1,0:T(8,128)(2,1)}, bf16[4,2,128,2048]{3,2,1,0:T(8,128)(2,1)}, u32[]{:S(2)}, u32[]{:S(2)}) collective-permute-start(bf16[4,2,128,2048]{3,2,1,0:T(8,128)(2,1)} %dynamic-slice_bitcast_fusion.1), channel_id=1, source_target_pairs={{0,4},{1,5},{2,6},{3,7},{4,0},{5,1},{6,2},{7,3},{8,12},{9,13},{10,... | collective-permute-start | bytes 12582920 | tf_op jit(solution)/shard_map/ppermute | solution.py:437
  507.3 174.4 %collective-permute-start.58 = (bf16[64,2048]{1,0:T(8,128)(2,1)}, bf16[64,2048]{1,0:T(8,128)(2,1)}, u32[]{:S(2)}, u32[]{:S(2)}) collective-permute-start(bf16[64,2048]{1,0:T(8,128)(2,1)} %slice.236), channel_id=1, source_target_pairs={{0,1},{1,0},{2,3},{3,2},{4,5},{5,4},{6,7},{7,6},{8,9},{9,8},{10,11... | collective-permute-start | bytes 786440 | tf_op jit(solution)/shard_map/ppermute | solution.py:433
  510.2 120.8 %collective-permute-start.57 = (bf16[2048,256]{1,0:T(8,128)(2,1)}, bf16[2048,256]{1,0:T(8,128)(2,1)}, u32[]{:S(2)}, u32[]{:S(2)}) collective-permute-start(bf16[2048,256]{1,0:T(8,128)(2,1)} %slice.258), channel_id=1, source_target_pairs={{0,1},{1,0},{2,3},{3,2},{4,5},{5,4},{6,7},{7,6},{8,9},{9,8},{10,11... | collective-permute-start | bytes 3145736 | tf_op jit(solution)/shard_map/ppermute | solution.py:433
  652.0 25.5 %collective-permute-start.53 = (bf16[128,2048]{1,0:T(8,128)(2,1)}, bf16[128,2048]{1,0:T(8,128)(2,1)}, u32[]{:S(2)}, u32[]{:S(2)}) collective-permute-start(bf16[128,2048]{1,0:T(8,128)(2,1)} %get-tuple-element.87), channel_id=1, source_target_pairs={{0,2},{1,3},{2,10},{3,11},{4,6},{5,7},{6,14},{7,15},{8,0},{9,1},{1... | collective-permute-start | bytes 1572872 | tf_op jit(solution)/shard_map/ppermute | solution.py:445
  654.5 91.9 %all-to-all-start.1 = ((bf16[32,64,448]{2,1,0:T(8,128)(2,1)}), bf16[32,64,448]{2,1,0:T(8,128)(2,1)S(1)}, u32[]{:S(2)}, u32[]{:S(2)}) async-start(bf16[32,64,448]{2,1,0:T(8,128)(2,1)} %pad_maximum_fusion.5), calls=%async_computation.1 | async-start | bytes 4194304 | tf_op jit(solution)/shard_map/all_to_all | solution.py:812
  658.5 84.6 %collective-permute-start.59 = (bf16[256,2048]{1,0:T(8,128)(2,1)}, bf16[256,2048]{1,0:T(8,128)(2,1)S(1)}, u32[]{:S(2)}, u32[]{:S(2)}) collective-permute-start(bf16[256,2048]{1,0:T(8,128)(2,1)} %slice.239), channel_id=1, source_target_pairs={{0,1},{1,0},{2,3},{3,2},{4,5},{5,4},{6,7},{7,6},{8,9},{9,8},{10,11... | collective-permute-start | bytes 3145736 | tf_op jit(solution)/shard_map/ppermute | solution.py:433
  662.7 48.2 %collective-permute-start.22 = (bf16[128,2048]{1,0:T(8,128)(2,1)S(1)}, bf16[128,2048]{1,0:T(8,128)(2,1)S(1)}, u32[]{:S(2)}, u32[]{:S(2)}) collective-permute-start(bf16[128,2048]{1,0:T(8,128)(2,1)S(1)} %get-tuple-element.92), channel_id=1, source_target_pairs={{0,8},{1,9},{2,0},{3,1},{4,12},{5,13},{6,4},{7,5},{8,16},{9,17},{1... | collective-permute-start | bytes 1572872 | tf_op jit(solution)/shard_map/ppermute | solution.py:441
  673.1 39.6 %collective-permute-start.26 = (bf16[128,2048]{1,0:T(8,128)(2,1)S(1)}, bf16[128,2048]{1,0:T(8,128)(2,1)S(1)}, u32[]{:S(2)}, u32[]{:S(2)}) collective-permute-start(bf16[128,2048]{1,0:T(8,128)(2,1)S(1)} %get-tuple-element.93), channel_id=1, source_target_pairs={{0,2},{1,3},{2,10},{3,11},{4,6},{5,7},{6,14},{7,15},{8,0},{9,1},{1... | collective-permute-start | bytes 1572872 | tf_op jit(solution)/shard_map/ppermute | solution.py:445
  679.8 49.9 %collective-permute-start.50 = (bf16[128,2048]{1,0:T(8,128)(2,1)S(1)}, bf16[128,2048]{1,0:T(8,128)(2,1)S(1)}, u32[]{:S(2)}, u32[]{:S(2)}) collective-permute-start(bf16[128,2048]{1,0:T(8,128)(2,1)S(1)} %get-tuple-element.84), channel_id=1, source_target_pairs={{0,8},{1,9},{2,0},{3,1},{4,12},{5,13},{6,4},{7,5},{8,16},{9,17},{1... | collective-permute-start | bytes 1572872 | tf_op jit(solution)/shard_map/ppermute | solution.py:441
  681.7 48.0 %collective-permute-start.54 = (bf16[128,2048]{1,0:T(8,128)(2,1)S(1)}, bf16[128,2048]{1,0:T(8,128)(2,1)S(1)}, u32[]{:S(2)}, u32[]{:S(2)}) collective-permute-start(bf16[128,2048]{1,0:T(8,128)(2,1)S(1)} %get-tuple-element.85), channel_id=1, source_target_pairs={{0,2},{1,3},{2,10},{3,11},{4,6},{5,7},{6,14},{7,15},{8,0},{9,1},{1... | collective-permute-start | bytes 1572872 | tf_op jit(solution)/shard_map/ppermute | solution.py:445
  740.9 27.0 %collective-permute-start.55 = (bf16[64,2048]{1,0:T(8,128)(2,1)S(1)}, bf16[64,2048]{1,0:T(8,128)(2,1)S(1)}, u32[]{:S(2)}, u32[]{:S(2)}) collective-permute-start(bf16[64,2048]{1,0:T(8,128)(2,1)S(1)} %get-tuple-element.98), channel_id=1, source_target_pairs={{0,1},{1,0},{2,3},{3,2},{4,5},{5,4},{6,7},{7,6},{8,9},{9,8},{10,11... | collective-permute-start | bytes 786440 | tf_op jit(solution)/shard_map/ppermute | solution.py:433
  742.6 26.2 %collective-permute-start.28 = (bf16[64,2048]{1,0:T(8,128)(2,1)S(1)}, bf16[64,2048]{1,0:T(8,128)(2,1)}, u32[]{:S(2)}, u32[]{:S(2)}) collective-permute-start(bf16[64,2048]{1,0:T(8,128)(2,1)S(1)} %get-tuple-element.106), channel_id=1, source_target_pairs={{0,1},{1,0},{2,3},{3,2},{4,5},{5,4},{6,7},{7,6},{8,9},{9,8},{10,11... | collective-permute-start | bytes 786440 | tf_op jit(solution)/shard_map/ppermute | solution.py:433
  (79 other events, 1554.7 us)
Sparse Core Ops, SparseCore 0:
  486.7 118.6 all-reduce.6
